TPU v7x, 32 devices: a whole 2x2x4 slice. The times are simulated.
32 devices in a mesh: layer: 2 (over y), row: 4 (over z), col: 4 (over x, core).
Axes of the slice: x: 2, y: 2, z: 4, core: 2. Of those that a mesh axis runs over, the one named last changes fastest.
Arguments:
- leaf_sol: bfloat16 [8, 256, 256], P(('layer', 'col'), 'row'), may hold values from -6 to 6
- lower_blocks: bfloat16 [8192, 1024], P(('layer', 'row'), 'col'), may hold values from -0.1875 to 0.1875
- lower_mask: int32 [32, 4], P(('layer', 'row'), 'col'), may hold values 0 or 1
- upper_blocks: bfloat16 [2048, 4096], P(('layer', 'col'), 'row'), may hold values from -0.125 to 0.125
- upper_mask: int32 [8, 16], P(('layer', 'col'), 'row'), may hold values 0 or 1
- anc_rhs: bfloat16 [4096, 256], P(('row', 'col')), may hold values from -6 to 6
- diag_inv: bfloat16 [4096, 256], P(('row', 'col')), may hold values from -0.375 to 0.375
Outputs:
- new_leaves: bfloat16 [8, 256, 256], P(('layer', 'col'), 'row')
- anc_sol: bfloat16 [4096, 256], P(('row', 'col'))
Inputs may be any that keep to these rules, and one draw needn't show every extreme that they name: `lower_mask`: 1 marks a stored block of L. `upper_mask`: 1 marks a stored block of U.
All inputs are finite; a program needn't handle non-finite values.
Results may differ from a plain program's by a relative error of at most 0.0044.
Values may be sent and summed in bfloat16 or wider, within the bound.
A program may use at most 64 MiB of HBM per device.

v0:
```python
import functools

import jax
import jax.numpy as jnp
from jax import lax
from jax.experimental import pallas as pl
from jax.experimental.pallas import tpu as pltpu
from jax.sharding import PartitionSpec as P

MESH = pl.DeviceIdType.MESH


def dot_last(a, b):
    return lax.dot_general(a, b, (((1,), (1,)), ((), ())), preferred_element_type=jnp.float32)


def kernel(
    n_layer, n_row, n_col, chunks,
    leaf, lower, lower_marks, upper, upper_marks, rhs, inv,
    new_leaves, anc_out,
    lower_mask, upper_mask, leaf_v, lower_v, upper_v, rhs_v, inv_v, x_all, x_t, rhs_t,
    pair_out, pair_in, held, part, part_in, anc_t, fold, fold_in,
    local_sem, x_send, x_recv, pair_send, pair_recv, part_send, part_recv,
    anc_send, pass_send, anc_recv, fold_send, fold_recv,
):
    layer = lax.axis_index("layer")
    row = lax.axis_index("row")
    col = lax.axis_index("col")
    halves = n_col // 2
    half, side = col // 2, lax.rem(col, 2)
    other = 1 - side
    partner = half * 2 + other
    block = inv_v.shape[0]
    width = rhs_v.shape[1]
    span = width // chunks
    share = span // n_layer
    strip = leaf_v.shape[0]
    depth = n_row * strip
    devices = n_layer * n_col
    group = [(dl, dh) for dl in range(n_layer) for dh in range(halves) if (dl, dh) != (0, 0)]

    def peer(dl, dh):
        return lax.rem(layer + dl, n_layer), lax.rem(half + dh, halves) * 2 + side

    barrier = pltpu.get_barrier_semaphore()
    for dr in reversed(range(1, n_row)):
        pl.semaphore_signal(barrier, inc=1, device_id=(layer, lax.rem(row + dr, n_row), col), device_id_type=MESH)
    for dl, dh in group:
        to_layer, to_col = peer(dl, dh)
        pl.semaphore_signal(barrier, inc=1, device_id=(to_layer, row, to_col), device_id_type=MESH)
    pl.semaphore_signal(barrier, inc=1, device_id=(layer, row, partner), device_id_type=MESH)
    loads = [
        pltpu.make_async_copy(source, target, local_sem.at[index])
        for index, (source, target) in enumerate(
            (
                (leaf.at[0], leaf_v), (lower, lower_v), (rhs, rhs_v), (inv, inv_v), (upper, upper_v),
                (lower_marks, lower_mask), (upper_marks, upper_mask),
            )
        )
    ]
    for load in loads:
        load.start()
    loads[0].wait()
    pl.semaphore_wait(barrier, n_row + len(group))

    def x_copy(j, to_row, from_row):
        return pltpu.make_async_remote_copy(
            src_ref=leaf_v.at[:, pl.ds(j * span, span)], dst_ref=x_all.at[j, from_row],
            send_sem=x_send.at[j * n_row + to_row], recv_sem=x_recv.at[j * n_row + from_row],
            device_id=(layer, to_row, col), device_id_type=MESH,
        )

    for j in range(chunks):
        for dr in range(1, n_row):
            x_copy(j, lax.rem(row + dr, n_row), row).start()
    for j in range(chunks):
        x_all[j, row] = leaf_v[:, j * span:(j + 1) * span]
    loads[2].wait()
    rhs_t[...] = rhs_v[...].astype(jnp.float32).T
    loads[1].wait()
    loads[3].wait()
    for load in loads[4:]:
        load.wait()
    strips = block // strip

    def partial_sum(j, to_col):
        total = None
        for k in range(depth // block):
            rows = lower_v[pl.ds(pl.multiple_of(to_col * block, block), block), k * block:(k + 1) * block]
            term = dot_last(x_t[j, k], rows) * lower_mask[k, to_col].astype(jnp.float32)
            total = term if total is None else total + term
        return total

    def pair_copy(j, h):
        return pltpu.make_async_remote_copy(
            src_ref=pair_out.at[j, h], dst_ref=pair_in.at[j, h],
            send_sem=pair_send.at[j * halves + h], recv_sem=pair_recv.at[j * halves + h],
            device_id=(layer, row, partner), device_id_type=MESH,
        )

    def inside(index):
        return pl.ds(pl.multiple_of(index * share, share), share)

    def part_copy(j, to_layer, to_col, from_layer, from_col):
        return pltpu.make_async_remote_copy(
            src_ref=part.at[j, to_col // 2, inside(to_layer)],
            dst_ref=part_in.at[j, from_layer * n_col + from_col],
            send_sem=part_send.at[j * devices + to_layer * n_col + to_col],
            recv_sem=part_recv.at[j * devices + from_layer * n_col + from_col],
            device_id=(to_layer, row, to_col), device_id_type=MESH,
        )

    for j in range(chunks):
        for dr in range(1, n_row):
            x_copy(j, row, lax.rem(row + dr, n_row)).wait_recv()
        for k in range(depth // block):
            x_t[j, k] = x_all[j, k * strips:(k + 1) * strips].reshape(block, span).T
        turns = [(dh, lax.rem(half + dh, halves)) for dh in reversed(range(halves))]
        for _, h in turns:
            pair_out[j, h] = partial_sum(j, h * 2 + other).astype(jnp.bfloat16)
            pair_copy(j, h).start()
        for _, h in turns:
            held[j, h] = partial_sum(j, h * 2 + side)
        for turn, h in turns:
            pair_copy(j, h).wait_recv()
            total = held[j, h] + pair_in[j, h].astype(jnp.float32)
            held[j, h] = total
            part[j, h] = total.astype(jnp.bfloat16)
            for dl, dh in reversed(group):
                if dh == turn:
                    part_copy(j, *peer(dl, dh), layer, col).start()

    def anc_place(j, from_layer, from_col):
        return anc_t.at[j, from_col, inside(from_layer)]

    def anc_copy(j, to_layer, to_col, from_layer, from_col):
        place = anc_place(j, from_layer, from_col)
        return pltpu.make_async_remote_copy(
            src_ref=place, dst_ref=place,
            send_sem=anc_send.at[j * devices + to_layer * n_col + to_col],
            recv_sem=anc_recv.at[j * devices + from_layer * n_col + from_col],
            device_id=(to_layer, row, to_col), device_id_type=MESH,
        )

    def pass_copy(j, from_layer, from_col):
        place = anc_place(j, from_layer, from_col)
        return pltpu.make_async_remote_copy(
            src_ref=place, dst_ref=place,
            send_sem=pass_send.at[j * devices + from_layer * n_col + from_col],
            recv_sem=anc_recv.at[j * devices + from_layer * n_col + from_col],
            device_id=(layer, row, partner), device_id_type=MESH,
        )

    inverse = inv_v[...]
    for j in range(chunks):
        remain = rhs_t[pl.ds(pl.multiple_of(j * span + layer * share, share), share), :] - held[j, half, inside(layer)]
        for dl, dh in group:
            from_layer, from_col = peer(dl, dh)
            part_copy(j, layer, col, from_layer, from_col).wait_recv()
            remain = remain - part_in[j, from_layer * n_col + from_col].astype(jnp.float32)
        high = remain.astype(jnp.bfloat16)
        rest = remain - high.astype(jnp.float32)
        middle = rest.astype(jnp.bfloat16)
        low = (rest - middle.astype(jnp.float32)).astype(jnp.bfloat16)
        terms = dot_last(jnp.concatenate([high, middle, low], axis=0), inverse)
        solved = terms[:share] + (terms[share:2 * share] + terms[2 * share:])
        anc_t[j, col, inside(layer)] = solved.astype(jnp.bfloat16)
        for dl, dh in reversed(group):
            anc_copy(j, *peer(dl, dh), layer, col).start()
        pass_copy(j, layer, col).start()

    def fold_copy(j, to_row, from_row):
        return pltpu.make_async_remote_copy(
            src_ref=fold.at[j, to_row], dst_ref=fold_in.at[j, from_row],
            send_sem=fold_send.at[j * n_row + to_row], recv_sem=fold_recv.at[j * n_row + from_row],
            device_id=(layer, to_row, col), device_id_type=MESH,
        )

    blocks_down = upper_v.shape[0] // block
    for j in range(chunks):
        for dl, dh in group:
            from_layer, from_col = peer(dl, dh)
            anc_copy(j, layer, col, from_layer, from_col).wait_recv()
            pass_copy(j, from_layer, from_col).start()
        totals = [None] * blocks_down
        for parity in (side, other):
            for dh in range(halves):
                from_col = lax.rem(half + dh, halves) * 2 + parity
                if parity is other:
                    for from_layer in range(n_layer):
                        pass_copy(j, from_layer, from_col).wait_recv()
                for i in range(blocks_down):
                    tile = upper_v[i * block:(i + 1) * block, pl.ds(pl.multiple_of(from_col * block, block), block)]
                    term = dot_last(tile, anc_t[j, from_col]) * upper_mask[i, from_col].astype(jnp.float32)
                    totals[i] = term if totals[i] is None else totals[i] + term
        for i in range(blocks_down):
            fold[j, i * strips:(i + 1) * strips] = totals[i].astype(jnp.bfloat16).reshape(strips, strip, span)
        for dr in range(1, n_row):
            fold_copy(j, lax.rem(row + dr, n_row), row).start()

    for j in range(chunks):
        anc_out[:, j * span:(j + 1) * span] = anc_t[j, col].T
    for j in range(chunks):
        correct = fold[j, row].astype(jnp.float32)
        for dr in range(1, n_row):
            from_row = lax.rem(row + dr, n_row)
            fold_copy(j, row, from_row).wait_recv()
            correct = correct + fold_in[j, from_row].astype(jnp.float32)
        columns = slice(j * span, (j + 1) * span)
        new_leaves[0, :, columns] = (leaf_v[:, columns].astype(jnp.float32) - correct).astype(jnp.bfloat16)

    for dr in range(1, n_row):
        for j in range(chunks):
            x_copy(j, lax.rem(row + dr, n_row), row).wait_send()
            fold_copy(j, lax.rem(row + dr, n_row), row).wait_send()
    for j in range(chunks):
        for h in range(halves):
            pair_copy(j, h).wait_send()
        pass_copy(j, layer, col).wait_send()
        for dl, dh in group:
            to_layer, to_col = peer(dl, dh)
            part_copy(j, to_layer, to_col, layer, col).wait_send()
            anc_copy(j, to_layer, to_col, layer, col).wait_send()
            pass_copy(j, to_layer, to_col).wait_send()


def finish(leaves, anc, leaves_out, anc_out, sem):
    copies = [
        pltpu.make_async_copy(anc, anc_out, sem.at[0]),
        pltpu.make_async_copy(leaves, leaves_out, sem.at[1]),
    ]
    for copy in copies:
        copy.start()
    for copy in copies:
        copy.wait()


def shards(n_layer, n_row, n_col, leaf_sol, lower_blocks, lower_mask, upper_blocks, upper_mask, anc_rhs, diag_inv):
    block = diag_inv.shape[1]
    width = leaf_sol.shape[2]
    strip = leaf_sol.shape[1]
    chunks = 2
    span = width // chunks
    share = span // n_layer
    halves = n_col // 2
    bf16, f32 = jnp.bfloat16, jnp.float32
    anywhere = pl.BlockSpec(memory_space=pltpu.HBM)
    lower_marks = lower_mask.T
    vmem = pl.BlockSpec(memory_space=pltpu.VMEM)
    devices = n_layer * n_col
    dma = lambda *sizes: [pltpu.SemaphoreType.DMA((size,)) for size in sizes]
    out_shape = (
        jax.ShapeDtypeStruct(leaf_sol.shape, bf16),
        jax.ShapeDtypeStruct(anc_rhs.shape, bf16),
    )
    results = pl.pallas_call(
        functools.partial(kernel, n_layer, n_row, n_col, chunks),
        out_shape=(pltpu.VMEM(leaf_sol.shape, bf16), pltpu.VMEM(anc_rhs.shape, bf16)),
        in_specs=[anywhere] * 7,
        out_specs=(vmem, vmem),
        scratch_shapes=[
            pltpu.SMEM(lower_marks.shape, jnp.int32),
            pltpu.SMEM(upper_mask.shape, jnp.int32),
            pltpu.VMEM((strip, width), bf16),
            pltpu.VMEM(lower_blocks.shape, bf16),
            pltpu.VMEM(upper_blocks.shape, bf16),
            pltpu.VMEM(anc_rhs.shape, bf16),
            pltpu.VMEM(diag_inv.shape, bf16),
            pltpu.VMEM((chunks, n_row, strip, span), bf16),
            pltpu.VMEM((chunks, n_row * strip // block, span, block), bf16),
            pltpu.VMEM((width, block), f32),
            pltpu.VMEM((chunks, halves, span, block), bf16),
            pltpu.VMEM((chunks, halves, span, block), bf16),
            pltpu.VMEM((chunks, halves, span, block), f32),
            pltpu.VMEM((chunks, halves, span, block), bf16),
            pltpu.VMEM((chunks, devices, share, block), bf16),
            pltpu.VMEM((chunks, n_col, span, block), bf16),
            pltpu.VMEM((chunks, n_row, strip, span), bf16),
            pltpu.VMEM((chunks, n_row, strip, span), bf16),
            *dma(
                7, chunks * n_row, chunks * n_row, chunks * halves, chunks * halves,
                *[chunks * devices] * 5, chunks * n_row, chunks * n_row,
            ),
        ],
        compiler_params=pltpu.CompilerParams(
            collective_id=0, has_side_effects=True,
        ),
    )(leaf_sol, lower_blocks, lower_marks, upper_blocks, upper_mask, anc_rhs, diag_inv)
    anyplace = pl.BlockSpec(memory_space=pl.ANY)
    return pl.pallas_call(
        finish,
        out_shape=out_shape,
        in_specs=[anyplace] * 2,
        out_specs=(anyplace, anyplace),
        scratch_shapes=dma(2),
        compiler_params=pltpu.CompilerParams(vmem_limit_bytes=1024 * 1024),
    )(*results)


def solution(mesh):
    in_specs = (
        P(("layer", "col"), "row", None),
        P(("layer", "row"), "col"),
        P(("layer", "row"), "col"),
        P(("layer", "col"), "row"),
        P(("layer", "col"), "row"),
        P(("row", "col"), None),
        P(("row", "col"), None),
    )
    out_specs = (P(("layer", "col"), "row", None), P(("row", "col"), None))
    body = functools.partial(shards, mesh.shape["layer"], mesh.shape["row"], mesh.shape["col"])
    return jax.shard_map(body, mesh=mesh, in_specs=in_specs, out_specs=out_specs, check_vma=False)
```

profile of v0, /device:TPU:0, one launch (start us, length us, event | category | flops | bytes accessed | tf_op | source)
XLA Modules:
  0.0 27.9 jit_solution(2638924167930905855)
XLA Ops:
  0.6 26.6 %shard_map.86 = (bf16[1,64,256]{2,1,0:T(8,128)(2,1)S(1)}, bf16[256,256]{1,0:T(8,128)(2,1)S(1)}) custom-call(bf16[1,64,256]{2,1,0:T(8,128)(2,1)} %leaf.1, bf16[1024,256]{1,0:T(8,128)(2,1)} %lower.1, s32[1,4]{1,0:T(1,128)} %bitcast.1, bf16[256,1024]{1,0:T(8,128)(2,1)} %upper.1, s32[1,4]{1,0:T(1,128)} %upper_marks.1, bf16[256,256]{1,0:T(8,128)(2,1)} %rhs.1, ...), custom_call_target="tpu_custom_call" | custom-call | tf_op jit(solution)/shard_map/pallas_call | solution.py:256
  27.2 0.7 %shard_map.87 = (bf16[1,64,256]{2,1,0:T(8,128)(2,1)}, bf16[256,256]{1,0:T(8,128)(2,1)}) custom-call(bf16[1,64,256]{2,1,0:T(8,128)(2,1)S(1)} %get-tuple-element.4.leaves, bf16[256,256]{1,0:T(8,128)(2,1)S(1)} %get-tuple-element.5.anc), custom_call_target="tpu_custom_call" | custom-call | tf_op jit(solution)/shard_map/pallas_call | solution.py:290
where the time goes:
time: 28.1 us; the launch traced here: 27.9 us
  Pallas kernels  27.3 us (97%)
  between operations  0.64 us (2%)
    pallas_call x1, Pallas kernels, shards(): pl.pallas_call(functools.partial(kernel, n_layer, n_row, n_col, chunks),...  26.6 us
    pallas_call x1, Pallas kernels, shards(): pl.pallas_call(finish, out_shape=out_shape, in_specs=[anyplace] * 2, out_...  0.68 us

commit v1 on v0

v1 whole, which is shorter than its diff:
```python
import contextlib
import functools

import jax
import jax.numpy as jnp
from jax import lax
from jax.experimental import pallas as pl
from jax.experimental.pallas import tpu as pltpu
from jax.sharding import PartitionSpec as P

MESH = pl.DeviceIdType.MESH
scope = lambda name: contextlib.nullcontext()


def dot_last(a, b):
    return lax.dot_general(a, b, (((1,), (1,)), ((), ())), preferred_element_type=jnp.float32)


def await_bytes(ref, sem):
    pltpu.make_async_copy(ref, ref, sem).wait()


def kernel(
    n_layer, n_row, n_col, chunks,
    leaf, lower, lower_marks, upper, upper_marks, rhs, inv,
    new_leaves, anc_out,
    lower_mask, upper_mask, leaf_v, lower_all, upper_all, rhs_all, inv_all, x_all, rhs_t,
    held, part, part_in, anc_t, anc_other, fold, fold_in,
    local_sem, pair_send, pair_recv, x_send, x_recv, part_send, part_recv,
    anc_send, anc_recv, fold_send, fold_recv, near,
):
    layer = lax.axis_index("layer")
    row = lax.axis_index("row")
    col = lax.axis_index("col")
    halves = n_col // 2
    shares = n_layer // 2
    half, side = col // 2, lax.rem(col, 2)
    other = 1 - side
    partner = half * 2 + other
    parity, quota = lax.rem(layer, 2), layer // 2
    block = inv.shape[0]
    strip, width = leaf_v.shape
    wide = width // 2
    span = wide // chunks
    share = span // shares
    depth = n_row * strip
    group = [
        (dh, dp, dq) for dh in reversed(range(halves)) for dp in reversed(range(2)) for dq in reversed(range(shares))
    ][:-1]

    def number(dh, dp, dq):
        return (dh * 2 + dp) * shares + dq - 1

    def back(dh, dp, dq):
        return (halves - dh) % halves, dp, (shares - dq) % shares

    def peer(dh, dp, dq):
        to_layer = lax.rem(quota + dq, shares) * 2 + lax.rem(layer + dp, 2)
        return to_layer, row, lax.rem(half + dh, halves) * 2 + side

    def straight(dh, dp, dq):
        return dh == 0 or (dp, dq) == (0, 0)

    barrier = pltpu.get_barrier_semaphore()

    def greet(*device):
        pl.semaphore_signal(barrier, inc=1, device_id=device, device_id_type=MESH)

    for dr in reversed(range(1, n_row)):
        greet(layer, lax.rem(row + dr, n_row), col)
        greet(layer, lax.rem(row + dr, n_row), partner)
    greet(layer, row, partner)
    straights = [step for step in group if straight(*step)]
    for step in straights:
        greet(*peer(*step))

    def columns(which):
        return pl.ds(pl.multiple_of(which * wide, wide), wide)

    loads = [
        pltpu.make_async_copy(source, target, local_sem.at[index])
        for index, (source, target) in enumerate(
            (
                (lower_marks, lower_mask), (lower, lower_all.at[0]), (upper_marks, upper_mask), (upper, upper_all.at[0]),
                (rhs.at[:, columns(side)], rhs_all.at[0]), (inv, inv_all.at[0]), (leaf.at[0], leaf_v),
                (leaf.at[0, :, columns(side)], x_all.at[side * n_row + row]),
            )
        )
    ]
    for load in loads:
        load.start()
    with scope("A_bar"):
        pl.semaphore_wait(barrier, 2 * (n_row - 1) + 1 + len(straights))

    def x_copy(dr, to_side):
        return pltpu.make_async_remote_copy(
            src_ref=leaf.at[0, :, columns(to_side)], dst_ref=x_all.at[side * n_row + row],
            send_sem=x_send.at[0], recv_sem=x_recv.at[0],
            device_id=(layer, lax.rem(row + dr, n_row), half * 2 + to_side), device_id_type=MESH,
        )

    for dr in reversed(range(n_row)):
        for to_side in (side, other) if dr else (other,):
            x_copy(dr, to_side).start()

    def pair_copy(index, source, target):
        return pltpu.make_async_remote_copy(
            src_ref=source, dst_ref=target, send_sem=pair_send.at[index], recv_sem=pair_recv.at[index],
            device_id=(layer, row, partner), device_id_type=MESH,
        )

    lower_pair = pair_copy(0, lower_all.at[0], lower_all.at[1])
    upper_pair = pair_copy(1, upper_all.at[0], upper_all.at[1])
    rhs_pair = pair_copy(2, rhs.at[:, columns(other)], rhs_all.at[1])
    inv_pair = pair_copy(3, inv, inv_all.at[1])
    rhs_pair.start()
    inv_pair.start()
    for step in straights:
        if step[0] == 0:
            pl.semaphore_signal(near, inc=1, device_id=peer(*step), device_id_type=MESH)

    def apply_marks(blocks, marks, transposed):
        for down in range(blocks.shape[1] // block):
            for across in range(blocks.shape[2] // block):
                place = 0, slice(down * block, (down + 1) * block), slice(across * block, (across + 1) * block)
                mark = marks[across, down] if transposed else marks[down, across]
                blocks[place] = blocks[place] * jnp.full((block, block), mark.astype(jnp.float32)).astype(jnp.bfloat16)

    with scope("B_lower"):
        loads[0].wait()
        loads[1].wait()
        apply_marks(lower_all, lower_mask, True)
        lower_pair.start()
    with scope("C_upper"):
        loads[2].wait()
        loads[3].wait()
        apply_marks(upper_all, upper_mask, False)
        upper_pair.start()
    with scope("D_rhs"):
        loads[4].wait()
        loads[5].wait()
        loads[6].wait()
        rhs_pair.wait_recv()
        inv_pair.wait_recv()
        chosen = lax.rem(layer + side, 2)
        rhs_t[...] = rhs_all[chosen].astype(jnp.float32).T
    with scope("E_lowerw"):
        lower_pair.wait_recv()
    with scope("F_xw"):
        loads[7].wait()
        await_bytes(x_all.at[pl.ds(0, 2 * n_row - 1)], x_recv.at[0])

    def x_turned(which):
        strips = x_all[pl.ds(which * n_row, n_row)].reshape(depth, wide)
        return [strips[k * block:(k + 1) * block].T for k in range(depth // block)]

    with scope("G_turn"):
        x_t = jnp.concatenate(x_turned(side) + x_turned(other), axis=1)

    def part_copy(j, dh, dp, dq):
        rows = pl.ds(pl.multiple_of(j * span + lax.rem(quota + dq, shares) * share, share), share)
        return pltpu.make_async_remote_copy(
            src_ref=part.at[dh * 2 + dp, rows], dst_ref=part_in.at[j, number(*back(dh, dp, dq))],
            send_sem=part_send.at[0], recv_sem=part_recv.at[j],
            device_id=peer(dh, dp, dq), device_id_type=MESH,
        )

    for dh in reversed(range(halves)):
        for dp in reversed(range(2)):
            with scope(f"H_mm{dh}{dp}"):
                b = lax.rem(half + dh, halves) * 2 + lax.rem(layer + dp, 2)
                rows = pl.ds(pl.multiple_of(b * block, block), block)
                total = dot_last(x_t, jnp.concatenate([lower_all[0, rows, :], lower_all[1, rows, :]], axis=1))
                if (dh, dp) == (0, 0):
                    held[...] = total
                if len(group) and (dh, dp) == group[0][:2]:
                    pl.semaphore_wait(near, sum(step[0] == 0 for step in straights))
                part[dh * 2 + dp] = total.astype(jnp.bfloat16)
                for step in group:
                    if step[:2] == (dh, dp):
                        part_copy(0, *step).start()
    for j in range(1, chunks):
        for step in group:
            part_copy(j, *step).start()

    own_block = half * 2 + parity

    def anc_copy(j, dh, dp, dq):
        place = anc_t.at[j, own_block, pl.ds(pl.multiple_of(quota * share, share), share)]
        return pltpu.make_async_remote_copy(
            src_ref=place, dst_ref=place,
            send_sem=anc_send.at[0], recv_sem=anc_recv.at[j * len(group) + number(*back(dh, dp, dq))],
            device_id=peer(dh, dp, dq), device_id_type=MESH,
        )

    def anc_arrival(j, dh, dp, dq):
        place = anc_t.at[j, own_block, pl.ds(0, share)]
        return await_bytes(place, anc_recv.at[j * len(group) + number(dh, dp, dq)])

    inverse = inv_all[chosen]
    for j in range(chunks):
        with scope(f"I{j}_partw"):
            await_bytes(part_in.at[j], part_recv.at[j])
        with scope(f"J{j}_solve"):
            rows = pl.ds(pl.multiple_of(j * span + quota * share, share), share)
            remain = rhs_t[rows, :] - held[rows, :]
            for index in range(len(group)):
                remain = remain - part_in[j, index].astype(jnp.float32)
            high = remain.astype(jnp.bfloat16)
            rest = remain - high.astype(jnp.float32)
            middle = rest.astype(jnp.bfloat16)
            low = (rest - middle.astype(jnp.float32)).astype(jnp.bfloat16)
            terms = dot_last(jnp.concatenate([high, middle, low], axis=0), inverse)
            solved = terms[:share] + (terms[share:2 * share] + terms[2 * share:])
            anc_t[j, own_block, pl.ds(pl.multiple_of(quota * share, share), share)] = solved.astype(jnp.bfloat16)
            for step in group:
                anc_copy(j, *step).start()
    with scope("K_upperw"):
        upper_pair.wait_recv()

    def fold_copy(j, dr, which):
        to_row = lax.rem(row + dr, n_row)
        return pltpu.make_async_remote_copy(
            src_ref=fold.at[j, which, to_row], dst_ref=fold_in.at[j, which * n_row + dr],
            send_sem=fold_send.at[0], recv_sem=fold_recv.at[j],
            device_id=(layer, to_row, partner if which else col), device_id_type=MESH,
        )

    anc_pair = [pair_copy(4 + j, anc_t.at[j, partner], anc_other.at[j]) for j in range(chunks)]
    blocks_down = upper_all.shape[1] // block
    strips = block // strip
    for j in range(chunks):
        totals = [[None] * blocks_down for _ in range(2)]
        for dh in range(halves):
            for dp in range(2):
                with scope(f"L{j}_ancw{dh}{dp}"):
                    for dq in range(shares):
                        if (dh, dp, dq) != (0, 0, 0):
                            anc_arrival(j, dh, dp, dq)
                with scope(f"M{j}_mm{dh}{dp}"):
                    b = lax.rem(half + dh, halves) * 2 + lax.rem(layer + dp, 2)
                    across = pl.ds(pl.multiple_of(b * block, block), block)
                    solved = anc_t[j, b]
                    for which in range(2):
                        for i in range(blocks_down):
                            term = dot_last(upper_all[which, i * block:(i + 1) * block, across], solved)
                            before = totals[which][i]
                            totals[which][i] = term if before is None else before + term
        with scope(f"N{j}_pack"):
            for which in range(2):
                for i in range(blocks_down):
                    for s in range(strips):
                        piece = totals[which][i][s * strip:(s + 1) * strip].reshape(chunks, strip // chunks, span)
                        fold[j, which, i * strips + s] = jnp.concatenate(
                            [piece[g] for g in range(chunks)], axis=1
                        ).astype(jnp.bfloat16)
            for dr in reversed(range(n_row)):
                for which in (0, 1) if dr else (1,):
                    fold_copy(j, dr, which).start()
            anc_pair[j].start()

    with scope("O_ancout"):
        for copy in anc_pair:
            copy.wait_recv()
        anc_out[:, columns(side)] = jnp.concatenate([anc_t[j, col] for j in range(chunks)], axis=0).T
        anc_out[:, columns(other)] = jnp.concatenate([anc_other[j] for j in range(chunks)], axis=0).T
    sums = []
    for j in range(chunks):
        with scope(f"P{j}_foldw"):
            await_bytes(fold_in.at[j, pl.ds(1, 2 * n_row - 1)], fold_recv.at[j])
        own = fold[j, 0, row].astype(jnp.float32)
        for dr in range(1, n_row):
            own = own + fold_in[j, dr].astype(jnp.float32)
        others = fold_in[j, n_row].astype(jnp.float32)
        for dr in range(1, n_row):
            others = others + fold_in[j, n_row + dr].astype(jnp.float32)
        sums.append((own, others))
    with scope("Q_out"):
        for which, target in enumerate((side, other)):
            correct = jnp.concatenate(
                [
                    jnp.concatenate([sums[j][which][:, g * span:(g + 1) * span] for j in range(chunks)], axis=1)
                    for g in range(chunks)
                ],
                axis=0,
            )
            new_leaves[0, :, columns(target)] = (leaf_v[:, columns(target)].astype(jnp.float32) - correct).astype(jnp.bfloat16)

    with scope("R_drain"):
        for copy in (lower_pair, upper_pair, rhs_pair, inv_pair, *anc_pair):
            copy.wait_send()
        await_bytes(x_all.at[pl.ds(0, 2 * n_row - 1)], x_send.at[0])
        await_bytes(part_in, part_send.at[0])
        await_bytes(part_in, anc_send.at[0])
        await_bytes(fold_in.at[:, pl.ds(1, 2 * n_row - 1)], fold_send.at[0])


def finish(leaves, anc, leaves_out, anc_out, sem):
    copies = [
        pltpu.make_async_copy(anc, anc_out, sem.at[0]),
        pltpu.make_async_copy(leaves, leaves_out, sem.at[1]),
    ]
    for copy in copies:
        copy.start()
    for copy in copies:
        copy.wait()


def shards(n_layer, n_row, n_col, leaf_sol, lower_blocks, lower_mask, upper_blocks, upper_mask, anc_rhs, diag_inv):
    block = diag_inv.shape[1]
    width = leaf_sol.shape[2]
    strip = leaf_sol.shape[1]
    chunks = 2
    wide = width // 2
    span = wide // chunks
    share = span // (n_layer // 2)
    peers = n_layer * n_col // 2 - 1
    bf16, f32 = jnp.bfloat16, jnp.float32
    anywhere = pl.BlockSpec(memory_space=pltpu.HBM)
    lower_marks = lower_mask.T
    vmem = pl.BlockSpec(memory_space=pltpu.VMEM)
    dma = lambda *sizes: [pltpu.SemaphoreType.DMA((size,)) for size in sizes]
    out_shape = (
        jax.ShapeDtypeStruct(leaf_sol.shape, bf16),
        jax.ShapeDtypeStruct(anc_rhs.shape, bf16),
    )
    results = pl.pallas_call(
        functools.partial(kernel, n_layer, n_row, n_col, chunks),
        out_shape=(pltpu.VMEM(leaf_sol.shape, bf16), pltpu.VMEM(anc_rhs.shape, bf16)),
        in_specs=[anywhere] * 7,
        out_specs=(vmem, vmem),
        scratch_shapes=[
            pltpu.SMEM(lower_marks.shape, jnp.int32),
            pltpu.SMEM(upper_mask.shape, jnp.int32),
            pltpu.VMEM((strip, width), bf16),
            pltpu.VMEM((2, *lower_blocks.shape), bf16),
            pltpu.VMEM((2, *upper_blocks.shape), bf16),
            pltpu.VMEM((2, block, wide), bf16),
            pltpu.VMEM((2, block, block), bf16),
            pltpu.VMEM((2 * n_row, strip, wide), bf16),
            pltpu.VMEM((wide, block), f32),
            pltpu.VMEM((wide, block), f32),
            pltpu.VMEM((n_col, wide, block), bf16),
            pltpu.VMEM((chunks, peers, share, block), bf16),
            pltpu.VMEM((chunks, n_col, span, block), bf16),
            pltpu.VMEM((chunks, span, block), bf16),
            pltpu.VMEM((chunks, 2, n_row, strip // chunks, wide), bf16),
            pltpu.VMEM((chunks, 2 * n_row, strip // chunks, wide), bf16),
            *dma(8, 4 + chunks, 4 + chunks, 1, 1, 1, chunks, 1, chunks * peers, 1, chunks),
            pltpu.SemaphoreType.REGULAR,
        ],
        compiler_params=pltpu.CompilerParams(
            collective_id=0, has_side_effects=True,
        ),
    )(leaf_sol, lower_blocks, lower_marks, upper_blocks, upper_mask, anc_rhs, diag_inv)
    anyplace = pl.BlockSpec(memory_space=pl.ANY)
    return pl.pallas_call(
        finish,
        out_shape=out_shape,
        in_specs=[anyplace] * 2,
        out_specs=(anyplace, anyplace),
        scratch_shapes=dma(2),
        compiler_params=pltpu.CompilerParams(vmem_limit_bytes=1024 * 1024),
    )(*results)


def solution(mesh):
    in_specs = (
        P(("layer", "col"), "row", None),
        P(("layer", "row"), "col"),
        P(("layer", "row"), "col"),
        P(("layer", "col"), "row"),
        P(("layer", "col"), "row"),
        P(("row", "col"), None),
        P(("row", "col"), None),
    )
    out_specs = (P(("layer", "col"), "row", None), P(("row", "col"), None))
    body = functools.partial(shards, mesh.shape["layer"], mesh.shape["row"], mesh.shape["col"])
    return jax.shard_map(body, mesh=mesh, in_specs=in_specs, out_specs=out_specs, check_vma=False)
```

time: 28.1 us -> 25.8 us (0.918)
  Pallas kernels: 27.3 us -> 25 us
    pallas_call x1, Pallas kernels: 26.6 us -> 24.3 us  [shards(): pl.pallas_call(functools.partial(kernel, n_layer, n_row, n_col, chunks),...]
where the time goes in v1:
time: 25.8 us; the launch traced here: 25.6 us
  Pallas kernels  25 us (97%)
  between operations  0.64 us (2%)
    pallas_call x1, Pallas kernels, shards(): pl.pallas_call(functools.partial(kernel, n_layer, n_row, n_col, chunks),...  24.3 us
    pallas_call x1, Pallas kernels, shards(): pl.pallas_call(finish, out_shape=out_shape, in_specs=[anyplace] * 2, out_...  0.68 us

profile of v1, /device:TPU:0, one launch (start us, length us, event | category | flops | bytes accessed | tf_op | source)
XLA Modules:
  0.0 25.6 jit_solution(7748728684782613367)
XLA Ops:
  0.6 24.3 %shard_map.86 = (bf16[1,64,256]{2,1,0:T(8,128)(2,1)S(1)}, bf16[256,256]{1,0:T(8,128)(2,1)S(1)}) custom-call(bf16[1,64,256]{2,1,0:T(8,128)(2,1)} %leaf.1, bf16[1024,256]{1,0:T(8,128)(2,1)} %lower.1, s32[1,4]{1,0:T(1,128)} %bitcast.1, bf16[256,1024]{1,0:T(8,128)(2,1)} %upper.1, s32[1,4]{1,0:T(1,128)} %upper_marks.1, bf16[256,256]{1,0:T(8,128)(2,1)} %rhs.1, ...), custom_call_target="tpu_custom_call" | custom-call | tf_op jit(solution)/shard_map/pallas_call | solution.py:327
  24.9 0.7 %shard_map.87 = (bf16[1,64,256]{2,1,0:T(8,128)(2,1)}, bf16[256,256]{1,0:T(8,128)(2,1)}) custom-call(bf16[1,64,256]{2,1,0:T(8,128)(2,1)S(1)} %get-tuple-element.4.leaves, bf16[256,256]{1,0:T(8,128)(2,1)S(1)} %get-tuple-element.5.anc), custom_call_target="tpu_custom_call" | custom-call | tf_op jit(solution)/shard_map/pallas_call | solution.py:357

commit v2 on v1

--- a/solution.py
+++ b/solution.py
@@ -16,18 +16,22 @@
     return lax.dot_general(a, b, (((1,), (1,)), ((), ())), preferred_element_type=jnp.float32)
 
 
+def dot(a, b):
+    return jnp.dot(a, b, preferred_element_type=jnp.float32)
+
+
 def await_bytes(ref, sem):
     pltpu.make_async_copy(ref, ref, sem).wait()
 
 
 def kernel(
-    n_layer, n_row, n_col, chunks,
+    n_layer, n_row, n_col, chunks, waves,
     leaf, lower, lower_marks, upper, upper_marks, rhs, inv,
     new_leaves, anc_out,
-    lower_mask, upper_mask, leaf_v, lower_all, upper_all, rhs_all, inv_all, x_all, rhs_t,
+    lower_mask, upper_mask, leaf_v, lower_v, lower_all, upper_all, rhs_all, inv_all, x_out, x_all, rhs_t,
     held, part, part_in, anc_t, anc_other, fold, fold_in,
     local_sem, pair_send, pair_recv, x_send, x_recv, part_send, part_recv,
-    anc_send, anc_recv, fold_send, fold_recv, near,
+    anc_send, anc_recv, fold_send, fold_recv, near, higher,
 ):
     layer = lax.axis_index("layer")
     row = lax.axis_index("row")
@@ -43,6 +47,8 @@
     wide = width // 2
     span = wide // chunks
     share = span // shares
+    batch = wide // waves
+    pack = wide // strip
     depth = n_row * strip
     group = [
         (dh, dp, dq) for dh in reversed(range(halves)) for dp in reversed(range(2)) for dq in reversed(range(shares))
@@ -66,9 +72,23 @@
     def greet(*device):
         pl.semaphore_signal(barrier, inc=1, device_id=device, device_id_type=MESH)
 
-    for dr in reversed(range(1, n_row)):
-        greet(layer, lax.rem(row + dr, n_row), col)
-        greet(layer, lax.rem(row + dr, n_row), partner)
+    def above(step):
+        return pl.when(row + step < n_row)
+
+    def below(step):
+        return pl.when(row >= step)
+
+    for step in reversed(range(1, n_row)):
+        @above(step)
+        def _():
+            greet(layer, row + step, col)
+            greet(layer, row + step, partner)
+
+    @below(1)
+    def _():
+        greet(layer, row - 1, col)
+        greet(layer, row - 1, partner)
+
     greet(layer, row, partner)
     straights = [step for step in group if straight(*step)]
     for step in straights:
@@ -81,27 +101,60 @@
         pltpu.make_async_copy(source, target, local_sem.at[index])
         for index, (source, target) in enumerate(
             (
-                (lower_marks, lower_mask), (lower, lower_all.at[0]), (upper_marks, upper_mask), (upper, upper_all.at[0]),
+                (lower_marks, lower_mask), (lower, lower_v), (upper_marks, upper_mask), (upper, upper_all.at[0]),
                 (rhs.at[:, columns(side)], rhs_all.at[0]), (inv, inv_all.at[0]), (leaf.at[0], leaf_v),
-                (leaf.at[0, :, columns(side)], x_all.at[side * n_row + row]),
             )
         )
     ]
-    for load in loads:
+    for load in reversed(loads):
         load.start()
+    with scope("A_leaf"):
+        loads[6].wait()
+        turned = leaf_v[...].T
+        for to_side in range(2):
+            for w in range(waves):
+                start = to_side * wide + w * batch
+                pieces = [turned[start + g * (batch // pack):start + (g + 1) * (batch // pack)] for g in range(pack)]
+                x_out[to_side, w] = jnp.concatenate(pieces, axis=1)
+        for w in range(waves):
+            x_all[w, side * n_row + row] = x_out[side, w]
     with scope("A_bar"):
-        pl.semaphore_wait(barrier, 2 * (n_row - 1) + 1 + len(straights))
-
-    def x_copy(dr, to_side):
-        return pltpu.make_async_remote_copy(
-            src_ref=leaf.at[0, :, columns(to_side)], dst_ref=x_all.at[side * n_row + row],
-            send_sem=x_send.at[0], recv_sem=x_recv.at[0],
-            device_id=(layer, lax.rem(row + dr, n_row), half * 2 + to_side), device_id_type=MESH,
-        )
-
-    for dr in reversed(range(n_row)):
-        for to_side in (side, other) if dr else (other,):
-            x_copy(dr, to_side).start()
+        pl.semaphore_wait(barrier, 2 * row + 2 * jnp.minimum(n_row - 1 - row, 1) + 1 + len(straights))
+
+    def x_copy(w, to_row, to_side, sem):
+        return pltpu.make_async_remote_copy(
+            src_ref=x_out.at[to_side, w], dst_ref=x_all.at[w, side * n_row + row],
+            send_sem=x_send.at[0], recv_sem=x_recv.at[2 * w + sem],
+            device_id=(layer, to_row, half * 2 + to_side), device_id_type=MESH,
+        )
+
+    def x_relay(w, from_side, step):
+        place = x_all.at[w, from_side * n_row + jnp.maximum(row - 1, 0)]
+        return pltpu.make_async_remote_copy(
+            src_ref=place, dst_ref=place, send_sem=x_send.at[1], recv_sem=x_recv.at[2 * w + 1],
+            device_id=(layer, row + step, col), device_id_type=MESH,
+        )
+
+    for w in range(waves):
+        for step in reversed(range(1, n_row)):
+            @below(step)
+            def _():
+                x_copy(w, row - step, side, 1).start()
+                x_copy(w, row - step, other, 1).start()
+
+        @above(1)
+        def _():
+            x_copy(w, row + 1, side, 0).start()
+            x_copy(w, row + 1, other, 0).start()
+
+        x_copy(w, row, other, 1).start()
+
+    def tell_below():
+        pl.semaphore_signal(higher, inc=1, device_id=(layer, row - 1, col), device_id_type=MESH)
+
+    @pl.when((row >= 1) & (row < n_row - 1))
+    def _():
+        tell_below()
 
     def pair_copy(index, source, target):
         return pltpu.make_async_remote_copy(
@@ -119,43 +172,70 @@
         if step[0] == 0:
             pl.semaphore_signal(near, inc=1, device_id=peer(*step), device_id_type=MESH)
 
-    def apply_marks(blocks, marks, transposed):
-        for down in range(blocks.shape[1] // block):
-            for across in range(blocks.shape[2] // block):
-                place = 0, slice(down * block, (down + 1) * block), slice(across * block, (across + 1) * block)
-                mark = marks[across, down] if transposed else marks[down, across]
-                blocks[place] = blocks[place] * jnp.full((block, block), mark.astype(jnp.float32)).astype(jnp.bfloat16)
+    def marked(tile, mark):
+        return tile * jnp.full((block, block), mark.astype(jnp.float32)).astype(jnp.bfloat16)
+
+    def blocks_of(ref):
+        rows, across = ref.shape
+        return [(down, over) for down in range(rows // block) for over in range(across // block)]
+
+    def at(down, over):
+        return slice(down * block, (down + 1) * block), slice(over * block, (over + 1) * block)
 
     with scope("B_lower"):
         loads[0].wait()
         loads[1].wait()
-        apply_marks(lower_all, lower_mask, True)
+        for down, over in blocks_of(lower_v):
+            lower_all[(0, *at(over, down))] = marked(lower_v[at(down, over)], lower_mask[over, down]).T
         lower_pair.start()
     with scope("C_upper"):
         loads[2].wait()
         loads[3].wait()
-        apply_marks(upper_all, upper_mask, False)
+        for down, over in blocks_of(upper):
+            place = (0, *at(down, over))
+            upper_all[place] = marked(upper_all[place], upper_mask[down, over])
         upper_pair.start()
+    def relay(w, step):
+        @pl.when((row >= 1) & (row + step < n_row))
+        def _():
+            for from_side in range(2):
+                x_relay(w, from_side, step).start()
+
+    for w in range(waves):
+        with scope(f"D_relay{w}"):
+            @below(1)
+            def _():
+                await_bytes(x_all.at[w, pl.ds(0, 2)], x_recv.at[2 * w])
+
+            relay(w, 1)
+            for step in range(2, n_row):
+                if w == 0:
+                    @above(step)
+                    def _():
+                        pl.semaphore_wait(higher, 1)
+
+                        @below(1)
+                        def _():
+                            tell_below()
+
+                relay(w, step)
+
     with scope("D_rhs"):
         loads[4].wait()
         loads[5].wait()
-        loads[6].wait()
         rhs_pair.wait_recv()
         inv_pair.wait_recv()
         chosen = lax.rem(layer + side, 2)
         rhs_t[...] = rhs_all[chosen].astype(jnp.float32).T
     with scope("E_lowerw"):
         lower_pair.wait_recv()
-    with scope("F_xw"):
-        loads[7].wait()
-        await_bytes(x_all.at[pl.ds(0, 2 * n_row - 1)], x_recv.at[0])
-
-    def x_turned(which):
-        strips = x_all[pl.ds(which * n_row, n_row)].reshape(depth, wide)
-        return [strips[k * block:(k + 1) * block].T for k in range(depth // block)]
-
-    with scope("G_turn"):
-        x_t = jnp.concatenate(x_turned(side) + x_turned(other), axis=1)
+    def x_turned(w, which):
+        strips = x_all[w, pl.ds(which * n_row, n_row)]
+        pieces = [
+            jnp.concatenate([strips[r][:, g * strip:(g + 1) * strip] for g in range(pack)], axis=0)
+            for r in range(n_row)
+        ]
+        return jnp.concatenate(pieces, axis=1)
 
     def part_copy(j, dh, dp, dq):
         rows = pl.ds(pl.multiple_of(j * span + lax.rem(quota + dq, shares) * share, share), share)
@@ -165,23 +245,45 @@
             device_id=peer(dh, dp, dq), device_id_type=MESH,
         )
 
-    for dh in reversed(range(halves)):
-        for dp in reversed(range(2)):
-            with scope(f"H_mm{dh}{dp}"):
-                b = lax.rem(half + dh, halves) * 2 + lax.rem(layer + dp, 2)
-                rows = pl.ds(pl.multiple_of(b * block, block), block)
-                total = dot_last(x_t, jnp.concatenate([lower_all[0, rows, :], lower_all[1, rows, :]], axis=1))
+    def product(x_own, x_else, dh, dp):
+        b = lax.rem(half + dh, halves) * 2 + lax.rem(layer + dp, 2)
+        across = pl.ds(pl.multiple_of(b * block, block), block)
+        return dot(x_own, lower_all[0, :, across]) + dot(x_else, lower_all[1, :, across])
+
+    near_count = sum(step[0] == 0 for step in straights)
+    x_t = []
+    for w in range(waves):
+        with scope(f"F{w}_xw"):
+            for r in range(n_row):
+                @pl.when(row == r)
+                def _():
+                    await_bytes(x_all.at[w, pl.ds(0, 2 * n_row - 1 - (2 if r else 0))], x_recv.at[2 * w + 1])
+        with scope(f"G{w}_turn"):
+            x_t.append((x_turned(w, side), x_turned(w, other)))
+        within = range(w * (chunks // waves), (w + 1) * (chunks // waves))
+        for dh in reversed(range(halves)):
+            for dp in reversed(range(2)):
                 if (dh, dp) == (0, 0):
-                    held[...] = total
-                if len(group) and (dh, dp) == group[0][:2]:
-                    pl.semaphore_wait(near, sum(step[0] == 0 for step in straights))
-                part[dh * 2 + dp] = total.astype(jnp.bfloat16)
+                    continue
+                with scope(f"H{w}_mm{dh}{dp}"):
+                    part[dh * 2 + dp, w * batch:(w + 1) * batch] = product(*x_t[w], dh, dp).astype(jnp.bfloat16)
+                    if w == 0 and (dh, dp) == group[0][:2]:
+                        pl.semaphore_wait(near, near_count)
+                    for step in group:
+                        if step[:2] == (dh, dp):
+                            part_copy(within[0], *step).start()
+        for j in within[1:]:
+            for step in group:
+                if step[:2] != (0, 0):
+                    part_copy(j, *step).start()
+    with scope("H_own"):
+        held[...] = product(*(jnp.concatenate(x, axis=0) for x in zip(*x_t)), 0, 0)
+        if shares > 1:
+            part[0] = held[...].astype(jnp.bfloat16)
+            for j in range(chunks):
                 for step in group:
-                    if step[:2] == (dh, dp):
-                        part_copy(0, *step).start()
-    for j in range(1, chunks):
-        for step in group:
-            part_copy(j, *step).start()
+                    if step[:2] == (0, 0):
+                        part_copy(j, *step).start()
 
     own_block = half * 2 + parity
 
@@ -189,13 +291,9 @@
         place = anc_t.at[j, own_block, pl.ds(pl.multiple_of(quota * share, share), share)]
         return pltpu.make_async_remote_copy(
             src_ref=place, dst_ref=place,
-            send_sem=anc_send.at[0], recv_sem=anc_recv.at[j * len(group) + number(*back(dh, dp, dq))],
+            send_sem=anc_send.at[0], recv_sem=anc_recv.at[j],
             device_id=peer(dh, dp, dq), device_id_type=MESH,
         )
-
-    def anc_arrival(j, dh, dp, dq):
-        place = anc_t.at[j, own_block, pl.ds(0, share)]
-        return await_bytes(place, anc_recv.at[j * len(group) + number(dh, dp, dq)])
 
     inverse = inv_all[chosen]
     for j in range(chunks):
@@ -226,26 +324,18 @@
             device_id=(layer, to_row, partner if which else col), device_id_type=MESH,
         )
 
-    anc_pair = [pair_copy(4 + j, anc_t.at[j, partner], anc_other.at[j]) for j in range(chunks)]
+    anc_pair = [pair_copy(4, anc_t.at[j, partner], anc_other.at[j]) for j in range(chunks)]
     blocks_down = upper_all.shape[1] // block
     strips = block // strip
     for j in range(chunks):
-        totals = [[None] * blocks_down for _ in range(2)]
-        for dh in range(halves):
-            for dp in range(2):
-                with scope(f"L{j}_ancw{dh}{dp}"):
-                    for dq in range(shares):
-                        if (dh, dp, dq) != (0, 0, 0):
-                            anc_arrival(j, dh, dp, dq)
-                with scope(f"M{j}_mm{dh}{dp}"):
-                    b = lax.rem(half + dh, halves) * 2 + lax.rem(layer + dp, 2)
-                    across = pl.ds(pl.multiple_of(b * block, block), block)
-                    solved = anc_t[j, b]
-                    for which in range(2):
-                        for i in range(blocks_down):
-                            term = dot_last(upper_all[which, i * block:(i + 1) * block, across], solved)
-                            before = totals[which][i]
-                            totals[which][i] = term if before is None else before + term
+        with scope(f"L{j}_ancw"):
+            await_bytes(part_in.at[j], anc_recv.at[j])
+        with scope(f"M{j}_mm"):
+            solved = jnp.concatenate([anc_t[j, b] for b in range(n_col)], axis=1)
+            totals = [
+                [dot_last(upper_all[which, i * block:(i + 1) * block, :], solved) for i in range(blocks_down)]
+                for which in range(2)
+            ]
         with scope(f"N{j}_pack"):
             for which in range(2):
                 for i in range(blocks_down):
@@ -260,8 +350,7 @@
             anc_pair[j].start()
 
     with scope("O_ancout"):
-        for copy in anc_pair:
-            copy.wait_recv()
+        await_bytes(anc_other, pair_recv.at[4])
         anc_out[:, columns(side)] = jnp.concatenate([anc_t[j, col] for j in range(chunks)], axis=0).T
         anc_out[:, columns(other)] = jnp.concatenate([anc_other[j] for j in range(chunks)], axis=0).T
     sums = []
@@ -287,9 +376,16 @@
             new_leaves[0, :, columns(target)] = (leaf_v[:, columns(target)].astype(jnp.float32) - correct).astype(jnp.bfloat16)
 
     with scope("R_drain"):
-        for copy in (lower_pair, upper_pair, rhs_pair, inv_pair, *anc_pair):
+        for copy in (lower_pair, upper_pair, rhs_pair, inv_pair):
             copy.wait_send()
-        await_bytes(x_all.at[pl.ds(0, 2 * n_row - 1)], x_send.at[0])
+        await_bytes(anc_other, pair_send.at[4])
+        for r in range(n_row):
+            @pl.when(row == r)
+            def _():
+                await_bytes(x_all.at[:, pl.ds(0, 2 * r + 1 + (2 if r < n_row - 1 else 0))], x_send.at[0])
+                if 0 < r < n_row - 1:
+                    await_bytes(x_all.at[:, pl.ds(0, 2 * (n_row - 1 - r))], x_send.at[1])
+
         await_bytes(part_in, part_send.at[0])
         await_bytes(part_in, anc_send.at[0])
         await_bytes(fold_in.at[:, pl.ds(1, 2 * n_row - 1)], fold_send.at[0])
@@ -310,7 +406,7 @@
     block = diag_inv.shape[1]
     width = leaf_sol.shape[2]
     strip = leaf_sol.shape[1]
-    chunks = 2
+    chunks, waves = 4, 2
     wide = width // 2
     span = wide // chunks
     share = span // (n_layer // 2)
@@ -325,7 +421,7 @@
         jax.ShapeDtypeStruct(anc_rhs.shape, bf16),
     )
     results = pl.pallas_call(
-        functools.partial(kernel, n_layer, n_row, n_col, chunks),
+        functools.partial(kernel, n_layer, n_row, n_col, chunks, waves),
         out_shape=(pltpu.VMEM(leaf_sol.shape, bf16), pltpu.VMEM(anc_rhs.shape, bf16)),
         in_specs=[anywhere] * 7,
         out_specs=(vmem, vmem),
@@ -333,11 +429,13 @@
             pltpu.SMEM(lower_marks.shape, jnp.int32),
             pltpu.SMEM(upper_mask.shape, jnp.int32),
             pltpu.VMEM((strip, width), bf16),
-            pltpu.VMEM((2, *lower_blocks.shape), bf16),
+            pltpu.VMEM(lower_blocks.shape, bf16),
+            pltpu.VMEM((2, *lower_blocks.shape[::-1]), bf16),
             pltpu.VMEM((2, *upper_blocks.shape), bf16),
             pltpu.VMEM((2, block, wide), bf16),
             pltpu.VMEM((2, block, block), bf16),
-            pltpu.VMEM((2 * n_row, strip, wide), bf16),
+            pltpu.VMEM((2, waves, strip // waves, wide), bf16),
+            pltpu.VMEM((waves, 2 * n_row, strip // waves, wide), bf16),
             pltpu.VMEM((wide, block), f32),
             pltpu.VMEM((wide, block), f32),
             pltpu.VMEM((n_col, wide, block), bf16),
@@ -346,7 +444,8 @@
             pltpu.VMEM((chunks, span, block), bf16),
             pltpu.VMEM((chunks, 2, n_row, strip // chunks, wide), bf16),
             pltpu.VMEM((chunks, 2 * n_row, strip // chunks, wide), bf16),
-            *dma(8, 4 + chunks, 4 + chunks, 1, 1, 1, chunks, 1, chunks * peers, 1, chunks),
+            *dma(7, 5, 5, 2, 2 * waves, 1, chunks, 1, chunks, 1, chunks),
+            pltpu.SemaphoreType.REGULAR,
             pltpu.SemaphoreType.REGULAR,
         ],
         compiler_params=pltpu.CompilerParams(

time: 25.8 us -> 25.2 us (0.977)
  Pallas kernels: 25 us -> 24.4 us
    pallas_call x1, Pallas kernels: 24.3 us -> 23.8 us  [shards(): pl.pallas_call(functools.partial(kernel, n_layer, n_row, n_col, chunks, w...]
where the time goes in v2:
time: 25.2 us; the launch traced here: 25.1 us
  Pallas kernels  24.4 us (97%)
  between operations  0.64 us (3%)
    pallas_call x1, Pallas kernels, shards(): pl.pallas_call(functools.partial(kernel, n_layer, n_row, n_col, chunks, w...  23.8 us
    pallas_call x1, Pallas kernels, shards(): pl.pallas_call(finish, out_shape=out_shape, in_specs=[anyplace] * 2, out_...  0.68 us

profile of v2, /device:TPU:0, one launch (start us, length us, event | category | flops | bytes accessed | tf_op | source)
XLA Modules:
  0.0 25.1 jit_solution(1826902762219635500)
XLA Ops:
  0.6 23.8 %shard_map.86 = (bf16[1,64,256]{2,1,0:T(8,128)(2,1)S(1)}, bf16[256,256]{1,0:T(8,128)(2,1)S(1)}) custom-call(bf16[1,64,256]{2,1,0:T(8,128)(2,1)} %leaf.1, bf16[1024,256]{1,0:T(8,128)(2,1)} %lower.1, s32[1,4]{1,0:T(1,128)} %bitcast.1, bf16[256,1024]{1,0:T(8,128)(2,1)} %upper.1, s32[1,4]{1,0:T(1,128)} %upper_marks.1, bf16[256,256]{1,0:T(8,128)(2,1)} %rhs.1, ...), custom_call_target="tpu_custom_call" | custom-call | tf_op jit(solution)/shard_map/pallas_call | solution.py:423
  24.4 0.7 %shard_map.87 = (bf16[1,64,256]{2,1,0:T(8,128)(2,1)}, bf16[256,256]{1,0:T(8,128)(2,1)}) custom-call(bf16[1,64,256]{2,1,0:T(8,128)(2,1)S(1)} %get-tuple-element.4.leaves, bf16[256,256]{1,0:T(8,128)(2,1)S(1)} %get-tuple-element.5.anc), custom_call_target="tpu_custom_call" | custom-call | tf_op jit(solution)/shard_map/pallas_call | solution.py:456

commit v3 on v2

--- a/solution.py
+++ b/solution.py
@@ -166,8 +166,6 @@
     upper_pair = pair_copy(1, upper_all.at[0], upper_all.at[1])
     rhs_pair = pair_copy(2, rhs.at[:, columns(other)], rhs_all.at[1])
     inv_pair = pair_copy(3, inv, inv_all.at[1])
-    rhs_pair.start()
-    inv_pair.start()
     for step in straights:
         if step[0] == 0:
             pl.semaphore_signal(near, inc=1, device_id=peer(*step), device_id_type=MESH)
@@ -194,7 +192,6 @@
         for down, over in blocks_of(upper):
             place = (0, *at(down, over))
             upper_all[place] = marked(upper_all[place], upper_mask[down, over])
-        upper_pair.start()
     def relay(w, step):
         @pl.when((row >= 1) & (row + step < n_row))
         def _():
@@ -223,10 +220,7 @@
     with scope("D_rhs"):
         loads[4].wait()
         loads[5].wait()
-        rhs_pair.wait_recv()
-        inv_pair.wait_recv()
         chosen = lax.rem(layer + side, 2)
-        rhs_t[...] = rhs_all[chosen].astype(jnp.float32).T
     with scope("E_lowerw"):
         lower_pair.wait_recv()
     def x_turned(w, which):
@@ -251,7 +245,7 @@
         return dot(x_own, lower_all[0, :, across]) + dot(x_else, lower_all[1, :, across])
 
     near_count = sum(step[0] == 0 for step in straights)
-    x_t = []
+    x_t, later = [], ()
     for w in range(waves):
         with scope(f"F{w}_xw"):
             for r in range(n_row):
@@ -261,6 +255,11 @@
         with scope(f"G{w}_turn"):
             x_t.append((x_turned(w, side), x_turned(w, other)))
         within = range(w * (chunks // waves), (w + 1) * (chunks // waves))
+        for j in later:
+            for step in group:
+                if step[:2] != (0, 0):
+                    part_copy(j, *step).start()
+        later = within[1:]
         for dh in reversed(range(halves)):
             for dp in reversed(range(2)):
                 if (dh, dp) == (0, 0):
@@ -272,10 +271,13 @@
                     for step in group:
                         if step[:2] == (dh, dp):
                             part_copy(within[0], *step).start()
-        for j in within[1:]:
-            for step in group:
-                if step[:2] != (0, 0):
-                    part_copy(j, *step).start()
+    for j in later:
+        for step in group:
+            if step[:2] != (0, 0):
+                part_copy(j, *step).start()
+    rhs_pair.start()
+    inv_pair.start()
+    upper_pair.start()
     with scope("H_own"):
         held[...] = product(*(jnp.concatenate(x, axis=0) for x in zip(*x_t)), 0, 0)
         if shares > 1:
@@ -295,6 +297,10 @@
             device_id=peer(dh, dp, dq), device_id_type=MESH,
         )
 
+    with scope("H_rhs"):
+        rhs_pair.wait_recv()
+        inv_pair.wait_recv()
+        rhs_t[...] = rhs_all[chosen].astype(jnp.float32).T
     inverse = inv_all[chosen]
     for j in range(chunks):
         with scope(f"I{j}_partw"):
@@ -333,7 +339,10 @@
         with scope(f"M{j}_mm"):
             solved = jnp.concatenate([anc_t[j, b] for b in range(n_col)], axis=1)
             totals = [
-                [dot_last(upper_all[which, i * block:(i + 1) * block, :], solved) for i in range(blocks_down)]
+                [
+                    dot_last(upper_all[which, i * block:(i + 1) * block, :], solved).astype(jnp.bfloat16)
+                    for i in range(blocks_down)
+                ]
                 for which in range(2)
             ]
         with scope(f"N{j}_pack"):
@@ -341,9 +350,7 @@
                 for i in range(blocks_down):
                     for s in range(strips):
                         piece = totals[which][i][s * strip:(s + 1) * strip].reshape(chunks, strip // chunks, span)
-                        fold[j, which, i * strips + s] = jnp.concatenate(
-                            [piece[g] for g in range(chunks)], axis=1
-                        ).astype(jnp.bfloat16)
+                        fold[j, which, i * strips + s] = jnp.concatenate([piece[g] for g in range(chunks)], axis=1)
             for dr in reversed(range(n_row)):
                 for which in (0, 1) if dr else (1,):
                     fold_copy(j, dr, which).start()
@@ -406,7 +413,7 @@
     block = diag_inv.shape[1]
     width = leaf_sol.shape[2]
     strip = leaf_sol.shape[1]
-    chunks, waves = 4, 2
+    chunks, waves = 2, 2
     wide = width // 2
     span = wide // chunks
     share = span // (n_layer // 2)

time: 25.2 us -> 24.9 us (0.988)
  Pallas kernels: 24.4 us -> 24.1 us
    pallas_call x1, Pallas kernels: 23.8 us -> 23.4 us  [shards(): pl.pallas_call(functools.partial(kernel, n_layer, n_row, n_col, chunks, w...]
where the time goes in v3:
time: 24.9 us; the launch traced here: 24.7 us
  Pallas kernels  24.1 us (97%)
  between operations  0.64 us (3%)
    pallas_call x1, Pallas kernels, shards(): pl.pallas_call(functools.partial(kernel, n_layer, n_row, n_col, chunks, w...  23.4 us
    pallas_call x1, Pallas kernels, shards(): pl.pallas_call(finish, out_shape=out_shape, in_specs=[anyplace] * 2, out_...  0.68 us

profile of v3, /device:TPU:0, one launch (start us, length us, event | category | flops | bytes accessed | tf_op | source)
XLA Modules:
  0.0 24.7 jit_solution(8420941803470749542)
XLA Ops:
  0.6 23.4 %shard_map.86 = (bf16[1,64,256]{2,1,0:T(8,128)(2,1)S(1)}, bf16[256,256]{1,0:T(8,128)(2,1)S(1)}) custom-call(bf16[1,64,256]{2,1,0:T(8,128)(2,1)} %leaf.1, bf16[1024,256]{1,0:T(8,128)(2,1)} %lower.1, s32[1,4]{1,0:T(1,128)} %bitcast.1, bf16[256,1024]{1,0:T(8,128)(2,1)} %upper.1, s32[1,4]{1,0:T(1,128)} %upper_marks.1, bf16[256,256]{1,0:T(8,128)(2,1)} %rhs.1, ...), custom_call_target="tpu_custom_call" | custom-call | tf_op jit(solution)/shard_map/pallas_call | solution.py:430
  24.1 0.7 %shard_map.87 = (bf16[1,64,256]{2,1,0:T(8,128)(2,1)}, bf16[256,256]{1,0:T(8,128)(2,1)}) custom-call(bf16[1,64,256]{2,1,0:T(8,128)(2,1)S(1)} %get-tuple-element.4.leaves, bf16[256,256]{1,0:T(8,128)(2,1)S(1)} %get-tuple-element.5.anc), custom_call_target="tpu_custom_call" | custom-call | tf_op jit(solution)/shard_map/pallas_call | solution.py:463

commit v4 on v3

--- a/solution.py
+++ b/solution.py
@@ -67,6 +67,8 @@
     def straight(dh, dp, dq):
         return dh == 0 or (dp, dq) == (0, 0)
 
+    leaf_load = pltpu.make_async_copy(leaf.at[0], leaf_v, local_sem.at[6])
+    leaf_load.start()
     barrier = pltpu.get_barrier_semaphore()
 
     def greet(*device):
@@ -102,14 +104,14 @@
         for index, (source, target) in enumerate(
             (
                 (lower_marks, lower_mask), (lower, lower_v), (upper_marks, upper_mask), (upper, upper_all.at[0]),
-                (rhs.at[:, columns(side)], rhs_all.at[0]), (inv, inv_all.at[0]), (leaf.at[0], leaf_v),
+                (rhs.at[:, columns(side)], rhs_all.at[0]), (inv, inv_all.at[0]),
             )
         )
     ]
-    for load in reversed(loads):
+    for load in loads:
         load.start()
     with scope("A_leaf"):
-        loads[6].wait()
+        leaf_load.wait()
         turned = leaf_v[...].T
         for to_side in range(2):
             for w in range(waves):

time: 24.9 us -> 24.7 us (level)
  no operation moved by 1% of the time
where the time goes in v4:
time: 24.7 us; the launch traced here: 24.6 us
  Pallas kernels  23.9 us (97%)
  between operations  0.64 us (3%)
    pallas_call x1, Pallas kernels, shards(): pl.pallas_call(functools.partial(kernel, n_layer, n_row, n_col, chunks, w...  23.3 us
    pallas_call x1, Pallas kernels, shards(): pl.pallas_call(finish, out_shape=out_shape, in_specs=[anyplace] * 2, out_...  0.68 us

profile of v4, /device:TPU:0, one launch (start us, length us, event | category | flops | bytes accessed | tf_op | source)
XLA Modules:
  0.0 24.6 jit_solution(561733966189401439)
XLA Ops:
  0.6 23.3 %shard_map.86 = (bf16[1,64,256]{2,1,0:T(8,128)(2,1)S(1)}, bf16[256,256]{1,0:T(8,128)(2,1)S(1)}) custom-call(bf16[1,64,256]{2,1,0:T(8,128)(2,1)} %leaf.1, bf16[1024,256]{1,0:T(8,128)(2,1)} %lower.1, s32[1,4]{1,0:T(1,128)} %bitcast.1, bf16[256,1024]{1,0:T(8,128)(2,1)} %upper.1, s32[1,4]{1,0:T(1,128)} %upper_marks.1, bf16[256,256]{1,0:T(8,128)(2,1)} %rhs.1, ...), custom_call_target="tpu_custom_call" | custom-call | tf_op jit(solution)/shard_map/pallas_call | solution.py:432
  23.9 0.7 %shard_map.87 = (bf16[1,64,256]{2,1,0:T(8,128)(2,1)}, bf16[256,256]{1,0:T(8,128)(2,1)}) custom-call(bf16[1,64,256]{2,1,0:T(8,128)(2,1)S(1)} %get-tuple-element.4.leaves, bf16[256,256]{1,0:T(8,128)(2,1)S(1)} %get-tuple-element.5.anc), custom_call_target="tpu_custom_call" | custom-call | tf_op jit(solution)/shard_map/pallas_call | solution.py:465
